TPU v7x, 32 devices: a whole 2x2x4 slice. The times are simulated.
32 devices in a mesh: samples: 16 (over z, y, core), feat: 2 (over x).
Axes of the slice: x: 2, y: 2, z: 4, core: 2. Of those that a mesh axis runs over, the one named last changes fastest.
Arguments:
- samples: float32 [4096, 4096], P('samples', 'feat'), may hold values from -12 to 12, as said below
- factor: float32 [4096, 512], P('feat'), may hold values from -6 to 6
Outputs:
- new_factor: float32 [4096, 512], P('feat')
Inputs may be any that keep to these rules, and one draw needn't show every extreme that they name: `samples`: Real-valued data.
All inputs are finite; a program needn't handle non-finite values.
Results may differ from a plain program's by a relative error of at most 0.00007.
Values sent between devices are 32-bit elements; how exact they have to be, the bound alone decides.
No kernel may reach another device: no remote copies, remote signals or barrier semaphores. Data moves between devices by JAX's collectives and lax.ppermute only.
A program may use at most 64 MiB of HBM per device.

v0:
```python
import jax
import jax.numpy as jnp
from jax import lax
from jax.sharding import PartitionSpec as P

D = 4096
R = 512


def per_device(samples, factor):
    high = lax.Precision.HIGHEST
    contract_rows = (((0,), (0,)), ((), ()))
    scaled = factor * (1.0 / jnp.sqrt(jnp.float32(D)))
    local_proj = jnp.dot(samples, scaled, precision=high, preferred_element_type=jnp.float32)
    proj = lax.psum(local_proj, "feat")
    squared = proj * proj
    rows_total = samples.shape[0] * lax.axis_size("samples")
    half_gram = lax.dot_general(
        scaled, scaled, contract_rows, precision=high, preferred_element_type=jnp.float32
    )
    gram = lax.psum(half_gram, "feat")
    squared_gram = gram * gram
    coef = 6.0 / jnp.sqrt(jnp.float32(D))
    local_moment = lax.dot_general(
        samples, squared, contract_rows, precision=high, preferred_element_type=jnp.float32
    )
    moment = lax.psum(local_moment, "samples") / rows_total
    gram_term = jnp.dot(scaled, squared_gram, precision=high, preferred_element_type=jnp.float32)
    grad = coef * (gram_term - moment)
    total = lax.psum(jnp.sum(grad * grad), "feat")
    rms = jnp.sqrt(total / (D * R)) + 1e-06
    return factor - 0.5 * grad / rms


def solution(mesh):
    placed = (P("samples", "feat"), P("feat", None))
    return jax.shard_map(
        per_device, mesh=mesh, in_specs=placed, out_specs=P("feat", None), check_vma=False
    )
```

profile of v0, /device:TPU:0, one launch (start us, length us, event | category | flops | bytes accessed | tf_op | source)
XLA Modules:
  0.0 228.2 jit_solution(14365884169956142107)
XLA Ops:
  6.5 0.0 copy-start
  6.5 0.0 all-reduce.6.cloned.1.call-start
  6.5 0.0 copy-start.1
  6.5 11.3 %fusion.4 = f32[512,512]{1,0:T(8,128)} fusion(f32[2048,512]{1,0:T(8,128)} %param.3), kind=kOutput, calls=%fused_computation.7 | convolution fusion | flops 6443499520 | bytes 5242880 | tf_op jit(solution)/shard_map/dot_general | solution.py:18
  17.8 0.0 copy-done
  17.8 0.0 copy-done.1
  17.9 7.5 %fusion.11 = f32[256,512]{0,1:T(8,128)} fusion(f32[256,2048]{1,0:T(8,128)S(1)} %copy-done, f32[2048,512]{1,0:T(8,128)S(1)} %copy-done.1), kind=kOutput, calls=%fused_computation.13 | convolution fusion | flops 3222274048 | bytes 6815744 | tf_op jit(solution)/shard_map/dot_general | solution.py:14
  25.4 0.0 all-reduce.6.cloned.1.call-update
  25.4 0.2 all-reduce.4.cloned.1.call-start
  25.6 54.2 %all-reduce.6.cloned.1.call-done = (f32[256,512]{0,1:T(8,128)}, f32[512,512]{1,0:T(8,128)}) async-done(((f32[256,512]{0,1:T(8,128)}, f32[512,512]{1,0:T(8,128)}), (f32[256,512]{0,1:T(8,128)}, f32[512,512]{1,0:T(8,128)})) %all-reduce.6.cloned.1.call-update) | async-done | bytes 1572880 | tf_op jit(solution)/shard_map/psum | solution.py:15
  79.8 6.1 %convolution_bitcast_fusion = f32[2048,512]{1,0:T(8,128)} fusion(f32[256,2048]{1,0:T(8,128)S(1)} %copy-done, f32[256,512]{0,1:T(8,128)} %get-tuple-element.5), kind=kOutput, calls=%fused_computation.9 | convolution fusion | flops 3221356544 | bytes 6815744 | tf_op jit(solution)/shard_map/dot_general | solution.py:24
  86.0 0.0 copy-start.2
  86.0 0.0 all-reduce.4.cloned.1.call-update
  86.0 111.2 %all-reduce.4.cloned.1.call-done = f32[2048,512]{1,0:T(8,128)} async-done(((f32[2048,512]{1,0:T(8,128)}), f32[2048,512]{1,0:T(8,128)}) %all-reduce.4.cloned.1.call-update) | async-done | bytes 4194320 | tf_op jit(solution)/shard_map/psum | solution.py:27
  197.2 0.0 copy-done.2
  197.2 11.5 %multiply_reduce_fusion = (f32[]{:T(128)}, f32[2048,512]{1,0:T(8,128)}) fusion(f32[2048,512]{1,0:T(8,128)} %all-reduce.4.cloned.1.call-done, f32[512,512]{1,0:T(8,128)S(1)} %copy-done.2, f32[2048,512]{1,0:T(8,128)} %param.3), kind=kOutput, calls=%fused_computation.1 | convolution fusion | flops 6449004544 | bytes 13631492 | tf_op jit(solution)/shard_map/dot_general | solution.py:28
  208.7 5.5 %psum.31 = f32[]{:T(128)} all-reduce(f32[]{:T(128)} %get-tuple-element.7), channel_id=1, replica_groups=mesh['samples'=16,'feat'=2] {'feat'}, use_global_device_ids=true, to_apply=%region_4.0 | all-reduce | flops 1 | bytes 8 | tf_op jit(solution)/shard_map/psum | solution.py:30
  214.9 6.5 %divide_subtract_fusion = f32[2048,512]{1,0:T(8,128)} fusion(f32[2048,512]{1,0:T(8,128)} %param.3, f32[2048,512]{1,0:T(8,128)} %get-tuple-element.8, f32[]{:T(128)S(6)} %add.11), kind=kLoop, calls=%fused_computation | loop fusion | flops 3145728 | bytes 12582916 | tf_op jit(solution)/shard_map/sub | solution.py:32
Async XLA Ops:
  6.5 11.3 %copy-start = (f32[256,2048]{1,0:T(8,128)S(1)}, f32[256,2048]{1,0:T(8,128)}, u32[]{:S(2)}) copy-start(f32[256,2048]{1,0:T(8,128)} %param.2) | copy-start | bytes 6291460
  6.5 73.3 %all-reduce.6.cloned.1.call-start = ((), (), s32[]{:S(2)}) async-start(), calls=%async_computation.1 | async-start | bytes 3145728 | tf_op jit(solution)/shard_map/psum | solution.py:15
  6.5 11.3 %copy-start.1 = (f32[2048,512]{1,0:T(8,128)S(1)}, f32[2048,512]{1,0:T(8,128)}, u32[]{:S(2)}) copy-start(f32[2048,512]{1,0:T(8,128)} %param.3) | copy-start | bytes 12582916
  25.4 171.8 %all-reduce.4.cloned.1.call-start = ((), (), s32[]{:S(2)}) async-start(), calls=%async_computation | async-start | bytes 8388608 | tf_op jit(solution)/shard_map/psum | solution.py:27
  86.0 111.2 %copy-start.2 = (f32[512,512]{1,0:T(8,128)S(1)}, f32[512,512]{1,0:T(8,128)}, u32[]{:S(2)}) copy-start(f32[512,512]{1,0:T(8,128)} %get-tuple-element.6) | copy-start | bytes 3145732
Sparse Core Ops, SparseCore 0:
  25.5 54.2 all-reduce.5
  86.1 111.0 all-reduce.3
where the time goes:
time: 228 us
  waiting for transfers between devices  165 us (72%)
  matrix products  36.5 us (16%)
  between operations  14 us (6%)
  other arithmetic  6.53 us (3%)
  blocking collectives  5.53 us (2%)
    psum x1, waiting for transfers between devices, per_device(): moment = lax.psum(local_moment, 'samples') / rows_total  111 us
    psum x1, waiting for transfers between devices, per_device(): proj = lax.psum(local_proj, 'feat')  54.2 us
    dot_general x1, matrix products, per_device(): jnp.dot(scaled, squared_gram, precision=high, preferred_element_type=jnp....  11.5 us
    dot_general x1, matrix products, per_device(): lax.dot_general(scaled, scaled, contract_rows, precision=high, preferred_...  11.3 us
    dot_general x1, matrix products, per_device(): jnp.dot(samples, scaled, precision=high, preferred_element_type=jnp.float32)  7.54 us
    sub x1, other arithmetic, per_device(): return factor - 0.5 * grad / rms  6.53 us
    dot_general x1, matrix products, per_device(): lax.dot_general(samples, squared, contract_rows, precision=high, preferre...  6.14 us
    psum x1, blocking collectives, per_device(): total = lax.psum(jnp.sum(grad * grad), 'feat')  5.53 us
  transfers between devices with their start and end apart: 2, of which 2 were waited for; matrix products, arithmetic and copies ran while one was open for 0% of the time, Pallas kernels for 0%

commit v1 on v0

--- a/solution.py
+++ b/solution.py
@@ -2,17 +2,23 @@
 import jax.numpy as jnp
 from jax import lax
 from jax.sharding import PartitionSpec as P
+from jax.lax import ppermute
 
 D = 4096
 R = 512
 
 
 def per_device(samples, factor):
+
+    def rest_stacks_all_now(tile_in, a_name):
+        block_next = ppermute(tile_in, a_name, [(0, 1), (1, 0)])
+        return tile_in + block_next
+
     high = lax.Precision.HIGHEST
     contract_rows = (((0,), (0,)), ((), ()))
     scaled = factor * (1.0 / jnp.sqrt(jnp.float32(D)))
     local_proj = jnp.dot(samples, scaled, precision=high, preferred_element_type=jnp.float32)
-    proj = lax.psum(local_proj, "feat")
+    proj = rest_stacks_all_now(local_proj, "feat")
     squared = proj * proj
     rows_total = samples.shape[0] * lax.axis_size("samples")
     half_gram = lax.dot_general(

time: 228 us -> 217 us (0.952)
  waiting for transfers between devices: 165 us -> 149 us
  starting transfers between devices: 0.22 us -> 3.26 us
    psum x1, waiting for transfers between devices: 54.2 us -> 13.2 us  [per_device(): gram = lax.psum(half_gram, 'feat')]
    ppermute x0 -> x1, waiting for transfers between devices: none -> 20.7 us  [rest_stacks_all_now(): block_next = ppermute(tile_in, a_name, [(0, 1), (1, 0)])]
    psum x1, waiting for transfers between devices: 111 us -> 115 us  [per_device(): moment = lax.psum(local_moment, 'samples') / rows_total]
    ppermute x0 -> x1, starting transfers between devices: none -> 3.04 us  [rest_stacks_all_now(): block_next = ppermute(tile_in, a_name, [(0, 1), (1, 0)])]
  transfers between devices with their start and end apart: 2 -> 3, of which waited for: 2 -> 3; matrix products, arithmetic and copies ran while one was open for 0% -> 6% of each run, Pallas kernels for 0% -> 0%
where the time goes in v1:
time: 217 us
  waiting for transfers between devices  149 us (69%)
  matrix products  37 us (17%)
  between operations  14.1 us (6%)
  other arithmetic  8.26 us (4%)
  blocking collectives  5.55 us (3%)
  starting transfers between devices  3.26 us (2%)
    psum x1, waiting for transfers between devices, per_device(): moment = lax.psum(local_moment, 'samples') / rows_total  115 us
    ppermute x1, waiting for transfers between devices, rest_stacks_all_now(): block_next = ppermute(tile_in, a_name, [(0, 1), (1, 0)])  20.7 us
    psum x1, waiting for transfers between devices, per_device(): gram = lax.psum(half_gram, 'feat')  13.2 us
    dot_general x1, matrix products, per_device(): jnp.dot(scaled, squared_gram, precision=high, preferred_element_type=jnp....  11.8 us
    dot_general x1, matrix products, per_device(): lax.dot_general(scaled, scaled, contract_rows, precision=high, preferred_...  11.3 us
    dot_general x1, matrix products, per_device(): jnp.dot(samples, scaled, precision=high, preferred_element_type=jnp.float32)  8.7 us
    sub x1, other arithmetic, per_device(): return factor - 0.5 * grad / rms  8.26 us
    psum x1, blocking collectives, per_device(): total = lax.psum(jnp.sum(grad * grad), 'feat')  5.55 us
  transfers between devices with their start and end apart: 3, of which 3 were waited for; matrix products, arithmetic and copies ran while one was open for 6% of the time, Pallas kernels for 0%

profile of v1, /device:TPU:0, one launch (start us, length us, event | category | flops | bytes accessed | tf_op | source)
XLA Modules:
  0.0 216.8 jit_solution(13439632795177544095)
XLA Ops:
  6.5 0.0 copy-start
  6.5 0.0 all-reduce.3.cloned.1.call-start
  6.5 11.3 %fusion.4 = f32[512,512]{1,0:T(8,128)} fusion(f32[2048,512]{1,0:T(8,128)} %param.3), kind=kOutput, calls=%fused_computation.7 | convolution fusion | flops 6443499520 | bytes 5242880 | tf_op jit(solution)/shard_map/dot_general | solution.py:24
  17.9 0.0 all-reduce.3.cloned.1.call-update
  17.9 0.2 all-reduce.5.cloned.1.call-start
  18.1 0.0 copy-done
  18.1 8.7 %fusion.9 = f32[256,512]{0,1:T(8,128)S(1)} fusion(f32[256,2048]{1,0:T(8,128)S(1)} %copy-done, f32[2048,512]{1,0:T(8,128)} %param.3), kind=kOutput, calls=%fused_computation.13 | convolution fusion | flops 3222274048 | bytes 6815744 | tf_op jit(solution)/shard_map/dot_general | solution.py:20
  26.9 3.0 %collective-permute-start = (f32[256,512]{0,1:T(8,128)S(1)}, f32[256,512]{0,1:T(8,128)S(1)}, u32[]{:S(2)}, u32[]{:S(2)}) collective-permute-start(f32[256,512]{0,1:T(8,128)S(1)} %fusion.9), channel_id=1, source_target_pairs={{0,1},{1,0},{2,3},{3,2},{4,5},{5,4},{6,7},{7,6},{8,9},{9,8},{10,11... | collective-permute-start | bytes 1572872 | tf_op jit(solution)/shard_map/ppermute | solution.py:14
  29.9 20.7 %collective-permute-done = f32[256,512]{0,1:T(8,128)S(1)} collective-permute-done((f32[256,512]{0,1:T(8,128)S(1)}, f32[256,512]{0,1:T(8,128)S(1)}, u32[]{:S(2)}, u32[]{:S(2)}) %collective-permute-start) | collective-permute-done | bytes 524320 | tf_op jit(solution)/shard_map/ppermute | solution.py:14
  50.6 5.2 %convolution_bitcast_fusion = f32[2048,512]{1,0:T(8,128)} fusion(f32[256,2048]{1,0:T(8,128)S(1)} %copy-done, f32[256,512]{0,1:T(8,128)S(1)} %fusion.9, f32[256,512]{0,1:T(8,128)S(1)} %collective-permute-done), kind=kOutput, calls=%fused_computation.9 | convolution fusion | flops 3221487616 | bytes 7340032 | tf_op jit(solution)/shard_map/dot_general | solution.py:30
  55.8 0.0 all-reduce.5.cloned.1.call-update
  55.8 13.2 %all-reduce.3.cloned.1.call-done = f32[512,512]{1,0:T(8,128)} async-done(((f32[512,512]{1,0:T(8,128)}), f32[512,512]{1,0:T(8,128)}) %all-reduce.3.cloned.1.call-update) | async-done | bytes 1048592 | tf_op jit(solution)/shard_map/psum | solution.py:27
  69.0 114.7 %all-reduce.5.cloned.1.call-done = f32[2048,512]{1,0:T(8,128)} async-done(((f32[2048,512]{1,0:T(8,128)}), f32[2048,512]{1,0:T(8,128)}) %all-reduce.5.cloned.1.call-update) | async-done | bytes 4194320 | tf_op jit(solution)/shard_map/psum | solution.py:33
  183.7 11.8 %multiply_reduce_fusion = (f32[]{:T(128)}, f32[2048,512]{1,0:T(8,128)}) fusion(f32[2048,512]{1,0:T(8,128)} %all-reduce.5.cloned.1.call-done, f32[512,512]{1,0:T(8,128)} %all-reduce.3.cloned.1.call-done, f32[2048,512]{1,0:T(8,128)} %param.3), kind=kOutput, calls=%fused_computation.1 | convolution fusion | flops 6449004544 | bytes 13631492 | tf_op jit(solution)/shard_map/dot_general | solution.py:34
  195.5 5.5 %psum.23 = f32[]{:T(128)} all-reduce(f32[]{:T(128)} %get-tuple-element.5), channel_id=1, replica_groups=mesh['samples'=16,'feat'=2] {'feat'}, use_global_device_ids=true, to_apply=%region_3.0 | all-reduce | flops 1 | bytes 8 | tf_op jit(solution)/shard_map/psum | solution.py:36
  201.7 8.3 %divide_subtract_fusion = f32[2048,512]{1,0:T(8,128)} fusion(f32[2048,512]{1,0:T(8,128)} %param.3, f32[]{:T(128)S(6)} %add.13, f32[2048,512]{1,0:T(8,128)} %get-tuple-element.6, f32[2048,512]{1,0:T(8,128)} %all-reduce.5.cloned.1.call-done), kind=kLoop, calls=%fused_computation | loop fusion | flops 5242880 | bytes 16777220 | tf_op jit(solution)/shard_map/sub | solution.py:38
Async XLA Ops:
  6.5 11.6 %copy-start = (f32[256,2048]{1,0:T(8,128)S(1)}, f32[256,2048]{1,0:T(8,128)}, u32[]{:S(2)}) copy-start(f32[256,2048]{1,0:T(8,128)} %param.2) | copy-start | bytes 6291460
  6.5 62.5 %all-reduce.3.cloned.1.call-start = ((), (), s32[]{:S(2)}) async-start(), calls=%async_computation | async-start | bytes 2097152 | tf_op jit(solution)/shard_map/psum | solution.py:27
  17.9 165.8 %all-reduce.5.cloned.1.call-start = ((), (), s32[]{:S(2)}) async-start(), calls=%async_computation.1 | async-start | bytes 8388608 | tf_op jit(solution)/shard_map/psum | solution.py:33
  26.9 23.7 %collective-permute-start = (f32[256,512]{0,1:T(8,128)S(1)}, f32[256,512]{0,1:T(8,128)S(1)}, u32[]{:S(2)}, u32[]{:S(2)}) collective-permute-start(f32[256,512]{0,1:T(8,128)S(1)} %fusion.9), channel_id=1, source_target_pairs={{0,1},{1,0},{2,3},{3,2},{4,5},{5,4},{6,7},{7,6},{8,9},{9,8},{10,11... | collective-permute-start | bytes 1572872 | tf_op jit(solution)/shard_map/ppermute | solution.py:14
Sparse Core Ops, SparseCore 0:
  18.0 50.9 all-reduce.2
  72.7 110.9 all-reduce.4
